TPU v7x, 256 devices: a whole 4x4x8 slice. The times are simulated.
256 devices in a mesh: dp: 8 (over z), fsdp: 16 (over x, y), tensor: 2 (over core).
Axes of the slice: x: 4, y: 4, z: 8, core: 2. Of those that a mesh axis runs over, the one named last changes fastest.
Arguments:
- tokens: bfloat16 [32768, 2048], P('fsdp'), may hold values from -6 to 6
- segment_ids: int32 [32768], P('fsdp'), may hold values from 0 to 127, never falling along the last dimension, each value on 1 to 512 neighbouring positions
- row_order: int32 [32768], P('fsdp'), may hold values from 0 to 2047, as said below
- row_counts: int32 [16], replicated, may hold values from 0 to 1280, as said below
- first_gain: float32 [2048], replicated, may hold values from 0.25 to 1.75
- second_gain: float32 [2048], replicated, may hold values from 0.25 to 1.75
- query_weight: bfloat16 [2048, 2048], P('fsdp', ('dp', 'tensor')), may hold values from -0.110485435 to 0.110485435
- key_weight: bfloat16 [2048, 2048], P('fsdp', ('dp', 'tensor')), may hold values from -4.4636116 to 4.4636116
- value_weight: bfloat16 [2048, 2048], P('fsdp', ('dp', 'tensor')), may hold values from -0.125 to 0.125
- output_weight: bfloat16 [2048, 2048], P(('dp', 'tensor'), 'fsdp'), may hold values from -0.125 to 0.125
- gate_weight: bfloat16 [2048, 8192], P('fsdp', ('dp', 'tensor')), may hold values from -0.125 to 0.125
- up_weight: bfloat16 [2048, 8192], P('fsdp', ('dp', 'tensor')), may hold values from -0.125 to 0.125
- down_weight: bfloat16 [8192, 2048], P(('dp', 'tensor'), 'fsdp'), may hold values from -0.0625 to 0.0625
Outputs:
- recursed: bfloat16 [32768, 2048], P('fsdp', ('dp', 'tensor'))
Inputs may be any that keep to these rules, and one draw needn't show every extreme that they name: `row_counts`: each entry is a multiple of 128, the entries sum to 16384, and the largest entry is exactly 1280. `row_order`: each shard's block of 2048 entries is a permutation of 0 to 2047.
All inputs are finite; a program needn't handle non-finite values.
Results may differ from a plain program's by a relative error of at most 0.015.
Values may be sent and summed in bfloat16 or wider, within the bound.
A program may use at most 128 MiB of HBM per device.

v0:
```python
import math
import jax
import jax.numpy as jnp
from jax import lax
from jax.sharding import PartitionSpec as P

TILE = 128


def rms_scale(row_data, gain_row):
    floats = row_data.astype(jnp.float32)
    inverse = lax.rsqrt(jnp.mean(floats * floats, axis=-1, keepdims=True) + 1e-05)
    return (floats * inverse * gain_row).astype(jnp.bfloat16)


def block_attention(queries, key_rows, value_rows, segments):
    row_total = queries.shape[0]
    block_len = math.gcd(row_total, 512)
    score_scale = 1.0 / math.sqrt(queries.shape[1])
    positions = jnp.arange(row_total, dtype=jnp.int32)

    def one_block(block_id):
        offset = block_id * block_len
        block_rows = lax.dynamic_slice_in_dim(queries, offset, block_len, 0)
        block_segs = lax.dynamic_slice_in_dim(segments, offset, block_len, 0)
        block_pos = offset + jnp.arange(block_len, dtype=jnp.int32)
        scores = (
            lax.dot_general(
                block_rows, key_rows, (((1,), (1,)), ((), ())), preferred_element_type=jnp.float32
            )
            * score_scale
        )
        allowed = (block_segs[:, None] == segments[None, :]) & (
            positions[None, :] <= block_pos[:, None]
        )
        scores = jnp.where(allowed, scores, -1e30)
        peak = jnp.max(scores, axis=-1, keepdims=True)
        expo = jnp.exp(scores - peak)
        probs = (expo / jnp.sum(expo, axis=-1, keepdims=True)).astype(jnp.bfloat16)
        return jnp.dot(probs, value_rows, preferred_element_type=jnp.float32).astype(jnp.bfloat16)

    outputs = lax.map(one_block, jnp.arange(row_total // block_len, dtype=jnp.int32))
    return outputs.reshape(row_total, queries.shape[1])


def feed_forward(ordered_cols, second_gain, gate_weight, up_weight, down_weight):
    full_rows = lax.all_gather(ordered_cols, ("dp", "tensor"), axis=1, tiled=True)
    normed = rms_scale(full_rows, second_gain)
    gate = jnp.dot(
        normed,
        lax.all_gather(gate_weight, "fsdp", axis=0, tiled=True),
        preferred_element_type=jnp.float32,
    )
    upward = jnp.dot(
        normed,
        lax.all_gather(up_weight, "fsdp", axis=0, tiled=True),
        preferred_element_type=jnp.float32,
    )
    hidden = (jax.nn.silu(gate) * upward).astype(jnp.bfloat16)
    terms = jnp.dot(
        hidden,
        lax.all_gather(down_weight, "fsdp", axis=1, tiled=True),
        preferred_element_type=jnp.float32,
    )
    return lax.psum_scatter(
        terms.astype(jnp.bfloat16), ("dp", "tensor"), scatter_dimension=1, tiled=True
    ).astype(jnp.float32)


def body(
    tokens,
    segment_ids,
    row_order,
    row_counts,
    first_gain,
    second_gain,
    query_weight,
    key_weight,
    value_weight,
    output_weight,
    gate_weight,
    up_weight,
    down_weight,
):
    normed = rms_scale(tokens, first_gain)
    weight_pieces = (
        lax.all_gather(query_weight, "fsdp", axis=0, tiled=True),
        lax.all_gather(key_weight, "fsdp", axis=0, tiled=True),
        lax.all_gather(value_weight, "fsdp", axis=0, tiled=True),
    )
    queries, key_rows, value_rows = tuple(
        (
            jnp.dot(normed, weight_piece, preferred_element_type=jnp.float32)
            for weight_piece in weight_pieces
        )
    )
    attended = block_attention(
        queries.astype(jnp.bfloat16),
        key_rows.astype(jnp.bfloat16),
        value_rows.astype(jnp.bfloat16),
        segment_ids,
    )
    head_terms = jnp.dot(
        attended,
        lax.all_gather(output_weight, "fsdp", axis=1, tiled=True),
        preferred_element_type=jnp.float32,
    )
    head_sum = lax.psum_scatter(
        head_terms.astype(jnp.bfloat16), ("dp", "tensor"), scatter_dimension=1, tiled=True
    ).astype(jnp.float32)
    share_cols = head_sum.shape[1]
    member = lax.axis_index(("dp", "tensor"))
    own_cols = lax.dynamic_slice_in_dim(tokens, member * share_cols, share_cols, 1)
    carried = (own_cols.astype(jnp.float32) + head_sum).astype(jnp.bfloat16)
    ordered = jnp.take(carried, row_order, axis=0)
    row_total = tokens.shape[0]
    live_count = lax.dynamic_index_in_dim(row_counts, lax.axis_index("fsdp"), 0, keepdims=False)
    is_live = jnp.arange(row_total, dtype=jnp.int32) < live_count
    own_tiles = row_total // TILE
    cap_rows = (own_tiles // 2 + own_tiles // 8) * TILE
    leading = ordered[:cap_rows]
    summed = feed_forward(leading, second_gain, gate_weight, up_weight, down_weight)
    finished = (leading.astype(jnp.float32) + summed).astype(jnp.bfloat16)
    updated = jnp.concatenate([finished, ordered[cap_rows:]], axis=0)
    token_rows = jnp.take(own_cols, row_order, axis=0)
    mixed = jnp.where(is_live[:, None], updated, token_rows)
    return own_cols.at[row_order].set(mixed)


def solution(mesh):
    in_specs = (
        P("fsdp", None),
        P("fsdp"),
        P("fsdp"),
        P(),
        P(),
        P(),
        P("fsdp", ("dp", "tensor")),
        P("fsdp", ("dp", "tensor")),
        P("fsdp", ("dp", "tensor")),
        P(("dp", "tensor"), "fsdp"),
        P("fsdp", ("dp", "tensor")),
        P("fsdp", ("dp", "tensor")),
        P(("dp", "tensor"), "fsdp"),
    )
    out_specs = P("fsdp", ("dp", "tensor"))
    return jax.shard_map(body, mesh=mesh, in_specs=in_specs, out_specs=out_specs, check_vma=False)
```

profile of v0, /device:TPU:2, one launch (start us, length us, event | category | flops | bytes accessed | tf_op | source)
XLA Modules:
  0.0 566.1 jit_solution(6179705660828530488)
XLA Ops:
  6.5 5.1 fusion.10
  11.7 24.0 %all_gather.26 = bf16[2048,128]{1,0:T(8,128)(2,1)S(1)} all-gather(bf16[128,128]{1,0:T(8,128)(2,1)S(1)} %copy-done.1), channel_id=1, replica_groups=mesh['dp'=8,'fsdp'=16,'tensor'=2] {'fsdp'}, dimensions={0}, use_global_device_ids=true | all-gather | bytes 557056 | tf_op jit(solution)/shard_map/all_gather | solution.py:89
  35.7 22.5 %all_gather.25 = bf16[2048,128]{1,0:T(8,128)(2,1)S(1)} all-gather(bf16[128,128]{1,0:T(8,128)(2,1)S(1)} %copy-done.2), channel_id=1, replica_groups=mesh['dp'=8,'fsdp'=16,'tensor'=2] {'fsdp'}, dimensions={0}, use_global_device_ids=true | all-gather | bytes 557056 | tf_op jit(solution)/shard_map/all_gather | solution.py:88
  58.2 8.6 %fusion.12 = bf16[2048,2048]{1,0:T(8,128)(2,1)} fusion(bf16[2048,2048]{1,0:T(8,128)(2,1)} %param.17, f32[2048]{0:T(1024)S(1)} %copy-done.7, f32[2048]{0:T(1024)S(1)} %add_rsqrt_fusion.1), kind=kLoop, calls=%fused_computation.21 | loop fusion | flops 16777216 | bytes 16793600 | tf_op jit(solution)/shard_map/convert_element_type | solution.py:13
  66.7 5.9 %convolution_convert_fusion.2 = bf16[2048,128]{1,0:T(8,128)(2,1)S(1)} fusion(bf16[2048,2048]{1,0:T(8,128)(2,1)} %fusion.12, bf16[2048,128]{1,0:T(8,128)(2,1)S(1)} %all_gather.26), kind=kOutput, calls=%fused_computation.31 | convolution fusion | flops 1074003968 | bytes 9437184 | tf_op jit(solution)/shard_map/dot_general | solution.py:93
  72.6 2.4 convolution_convert_fusion.3
  75.0 22.8 %all_gather.24 = bf16[2048,128]{1,0:T(8,128)(2,1)S(1)} all-gather(bf16[128,128]{1,0:T(8,128)(2,1)S(1)} %copy-done.3), channel_id=1, replica_groups=mesh['dp'=8,'fsdp'=16,'tensor'=2] {'fsdp'}, dimensions={0}, use_global_device_ids=true | all-gather | bytes 557056 | tf_op jit(solution)/shard_map/all_gather | solution.py:87
  97.8 2.4 convolution_convert_fusion.4
  100.3 17.5 %while.11 = (s32[]{:T(128)}, bf16[4,512,128]{2,1,0:T(8,128)(2,1)S(1)}, s32[4]{0:T(128)S(1)}, s32[2048]{0:T(1024)S(1)}, bf16[2048,128]{1,0:T(8,128)(2,1)S(1)}, /*...) while((s32[]{:T(128)}, ...), condition=%wide.region_4.5_spmd.clone, body=%wide.region_1.4_spmd.clone.sunk | while | flops 548470272 | bytes 13922487 | solution.py:42
  117.8 23.1 %all_gather.27 = bf16[128,2048]{1,0:T(8,128)(2,1)S(1)} all-gather(bf16[128,128]{1,0:T(8,128)(2,1)S(1)} %copy-done.4), channel_id=1, replica_groups=mesh['dp'=8,'fsdp'=16,'tensor'=2] {'fsdp'}, dimensions={1}, use_global_device_ids=true | all-gather | bytes 557056 | tf_op jit(solution)/shard_map/all_gather | solution.py:105
  140.8 5.6 convolution_convert_fusion.1
  146.4 12.3 %copy.14 = bf16[2048,2048]{0,1:T(8,128)(2,1)} copy(bf16[2048,2048]{1,0:T(8,128)(2,1)} %convolution_convert_fusion.1) | data formatting | bytes 16777216
  159.4 71.6 %reduce-scatter.7.cloned.1.call-done = bf16[128,2048]{1,0:T(8,128)(2,1)} async-done(((bf16[2048,2048]{1,0:T(8,128)(2,1)}), bf16[128,2048]{1,0:T(8,128)(2,1)}) %reduce-scatter.7.cloned.1.call-update) | async-done | bytes 524304
  234.3 6.2 %gather_fusion = bf16[2048,128]{1,0:T(8,128)(2,1)S(1)} fusion(bf16[2048,128]{1,0:T(8,128)(2,1)S(1)} %get-tuple-element.79, s32[2048]{0:T(1024)S(1)} %get-tuple-element.83), kind=kCustom, calls=%fused_computation.clone | custom fusion | bytes 1056768 | tf_op jit(solution)/shard_map/jit(_take)/gather | solution.py:115
  243.8 49.9 %all-gather.5.cloned.1.call-done = bf16[1280,2048]{1,0:T(8,128)(2,1)} async-done(((bf16[1280,128]{1,0:T(8,128)(2,1)}), bf16[1280,2048]{1,0:T(8,128)(2,1)}) %all-gather.5.cloned.1.call-update) | async-done | bytes 5242896 | tf_op jit(solution)/shard_map/all_gather | solution.py:47
  293.7 3.6 fusion.13
  297.3 47.7 %all-gather.7.cloned.1.call-done = bf16[2048,512]{1,0:T(8,128)(2,1)} async-done(((bf16[128,512]{1,0:T(8,128)(2,1)}), bf16[2048,512]{1,0:T(8,128)(2,1)}) %all-gather.7.cloned.1.call-update) | async-done | bytes 2097168 | tf_op jit(solution)/shard_map/all_gather | solution.py:51
  345.0 7.6 %fusion.18 = f32[1280,512]{1,0:T(8,128)} fusion(bf16[2048,512]{1,0:T(8,128)(2,1)} %all-gather.7.cloned.1.call-done, bf16[1280,2048]{1,0:T(8,128)(2,1)} %all-gather.5.cloned.1.call-done, f32[2048]{0:T(1024)S(1)} %copy-done.8, f32[1280]{0:T(1024)S(1)} %add_rsqrt_fusion), kind=kOutput, calls=%fused_computation.34 | convolution fusion | flops 2694840320 | bytes 9974784 | tf_op jit(solution)/shard_map/dot_general | solution.py:49
  352.6 46.1 %all-gather.11.cloned.1.call-done = bf16[512,2048]{1,0:T(8,128)(2,1)} async-done(((bf16[512,128]{1,0:T(8,128)(2,1)}), bf16[512,2048]{1,0:T(8,128)(2,1)}) %all-gather.11.cloned.1.call-update) | async-done | bytes 2097168 | tf_op jit(solution)/shard_map/all_gather | solution.py:62
  398.7 51.6 %all-gather.9.cloned.1.call-done = bf16[2048,512]{1,0:T(8,128)(2,1)} async-done(((bf16[128,512]{1,0:T(8,128)(2,1)}), bf16[2048,512]{1,0:T(8,128)(2,1)}) %all-gather.9.cloned.1.call-update) | async-done | bytes 2097168 | tf_op jit(solution)/shard_map/all_gather | solution.py:56
  450.4 11.2 %convolution_convert_fusion = bf16[1280,2048]{1,0:T(8,128)(2,1)} fusion(bf16[512,2048]{1,0:T(8,128)(2,1)} %all-gather.11.cloned.1.call-done, bf16[2048,512]{1,0:T(8,128)(2,1)} %all-gather.9.cloned.1.call-done, f32[1280,512]{1,0:T(8,128)} %fusion.18, bf16[1280,2048]{1,0:T(8,128)(2,1)} %all-gather.5.cloned.1.call-done, f32[2048]{0:T(1024)S(1)} %copy-done.8, ...), kind=kOutput, calls=%fused_computation.27 | convolution fusion | flops 5385748480 | bytes 17314816 | tf_op jit(solution)/shard_map/dot_general | solution.py:60
  461.6 7.9 %copy.16 = bf16[1280,2048]{0,1:T(8,128)(2,1)} copy(bf16[1280,2048]{1,0:T(8,128)(2,1)} %convolution_convert_fusion) | data formatting | bytes 10485760
  471.3 63.3 %reduce-scatter.9.cloned.1.call-done = bf16[128,1280]{1,0:T(8,128)(2,1)} async-done(((bf16[2048,1280]{1,0:T(8,128)(2,1)}), bf16[128,1280]{1,0:T(8,128)(2,1)}) %reduce-scatter.9.cloned.1.call-update) | async-done | bytes 327696
  535.9 23.4 %scatter_custom_fusion = bf16[2048,128]{1,0:T(8,128)(2,1)} fusion(bf16[2048,128]{1,0:T(8,128)(2,1)} %get-tuple-element.80, s32[2048]{0:T(1024)S(1)} %get-tuple-element.84, bf16[768,128]{1,0:T(8,128)(2,1)S(1)} %slice.13, bf16[]{:T(256)} %constant.75, bf16[1280,128]{1,0:T(8,128)(2,1)S(1)} %add_convert_fusion.1, pred[2048]{0:T(1024)(128)(4,1)S(1)} %compare_and_fusion, ...), kind=kCustom, calls=%fused_computation.39 | custom fusion | flops 1572864 | bytes 1585156 | tf_op jit(solution)/shard_map/scatter | solution.py:127
  (71 shorter events, 25.1 us)
Async XLA Ops:
  6.5 5.1 copy-start.1
  6.5 29.1 %copy-start.2 = (bf16[128,128]{1,0:T(8,128)(2,1)S(1)}, bf16[128,128]{1,0:T(8,128)(2,1)}, u32[]{:S(2)}) copy-start(bf16[128,128]{1,0:T(8,128)(2,1)} %param.24) | copy-start | bytes 98308
  6.5 51.6 %copy-start.7 = (f32[2048]{0:T(1024)S(1)}, f32[2048]{0:T(1024)}, u32[]{:S(2)}) copy-start(f32[2048]{0:T(1024)} %param.21) | copy-start | bytes 24580
  6.5 224.5 %reduce-scatter.7.cloned.1.call-start = ((), (), s32[]{:S(2)}) async-start(), calls=%async_computation.6 | async-start | bytes 8912896
  66.7 5.9 %copy-start = (bf16[2048,2048]{1,0:T(8,128)(2,1)S(1)}, bf16[2048,2048]{1,0:T(8,128)(2,1)}, u32[]{:S(2)}) copy-start(bf16[2048,2048]{1,0:T(8,128)(2,1)} %fusion.12) | copy-start | bytes 25165828
  72.6 2.4 copy-start.3
  97.8 2.4 copy-start.6
  100.3 17.5 %copy-start.4 = (bf16[128,128]{1,0:T(8,128)(2,1)S(1)}, bf16[128,128]{1,0:T(8,128)(2,1)}, u32[]{:S(2)}) copy-start(bf16[128,128]{1,0:T(8,128)(2,1)} %param.26) | copy-start | bytes 98308
  158.7 0.7 copy-start.5
  158.7 135.0 %all-gather.5.cloned.1.call-start = ((), (), s32[]{:S(2)}) async-start(), calls=%async_computation.2 | async-start | bytes 5570560 | tf_op jit(solution)/shard_map/all_gather | solution.py:47
  234.3 110.7 %copy-start.8 = (f32[2048]{0:T(1024)S(1)}, f32[2048]{0:T(1024)}, u32[]{:S(2)}) copy-start(f32[2048]{0:T(1024)} %param.22) | copy-start | bytes 24580
  241.6 103.4 %all-gather.7.cloned.1.call-start = ((), (), s32[]{:S(2)}) async-start(), calls=%async_computation.3 | async-start | bytes 2228224 | tf_op jit(solution)/shard_map/all_gather | solution.py:51
  242.3 156.4 %all-gather.11.cloned.1.call-start = ((), (), s32[]{:S(2)}) async-start(), calls=%async_computation.5 | async-start | bytes 2228224 | tf_op jit(solution)/shard_map/all_gather | solution.py:62
  242.9 207.5 %all-gather.9.cloned.1.call-start = ((), (), s32[]{:S(2)}) async-start(), calls=%async_computation.4 | async-start | bytes 2228224 | tf_op jit(solution)/shard_map/all_gather | solution.py:56
  243.5 291.1 %reduce-scatter.9.cloned.1.call-start = ((), (), s32[]{:S(2)}) async-start(), calls=%async_computation.7 | async-start | bytes 5570560
  469.5 0.7 copy-start.9
Sparse Core Ops, SparseCore 0:
  158.8 72.1 reduce-scatter.6
  241.7 51.9 all-gather.4
  296.1 48.8 all-gather.6
  347.3 51.4 all-gather.10
  401.0 49.3 all-gather.8
  469.6 64.9 reduce-scatter.8
where the time goes:
time: 567 us; the launch traced here: 566 us
  waiting for transfers between devices  332 us (59%)
  blocking collectives  92.4 us (16%)
  other arithmetic  46.5 us (8%)
  matrix products  44.3 us (8%)
  local copies, waits for them, and re-layouts  34.2 us (6%)
  between operations  13.7 us (2%)
    unnamed x8, waiting for transfers between devices  137 us
    all_gather x1, waiting for transfers between devices, feed_forward(): lax.all_gather(up_weight, 'fsdp', axis=0, tiled=True)  51.6 us
    all_gather x1, waiting for transfers between devices, feed_forward(): lax.all_gather(ordered_cols, ('dp', 'tensor'), axis=1, tiled=True)  49.9 us
    all_gather x1, waiting for transfers between devices, feed_forward(): lax.all_gather(gate_weight, 'fsdp', axis=0, tiled=True)  47.7 us
    all_gather x1, waiting for transfers between devices, feed_forward(): lax.all_gather(down_weight, 'fsdp', axis=1, tiled=True)  46.1 us
    all_gather x1, blocking collectives, body(): lax.all_gather(value_weight, 'fsdp', axis=0, tiled=True)  24 us
    unnamed x24, local copies, waits for them, and re-layouts  23.9 us
    scatter x1, other arithmetic, body(): return own_cols.at[row_order].set(mixed)  23.4 us
  transfers between devices with their start and end apart: 6, of which 6 were waited for; matrix products, arithmetic and copies ran while one was open for 2% of the time, Pallas kernels for 0%

commit v1 on v0

--- a/solution.py
+++ b/solution.py
@@ -3,6 +3,7 @@
 import jax.numpy as jnp
 from jax import lax
 from jax.sharding import PartitionSpec as P
+from jax.lax import all_to_all, axis_size
 
 TILE = 128
 
@@ -57,10 +58,17 @@
         preferred_element_type=jnp.float32,
     )
     hidden = (jax.nn.silu(gate) * upward).astype(jnp.bfloat16)
+
+    def process_sheet_in(piece_in, which_axis):
+        bank = []
+        for _ in range(axis_size(which_axis)):
+            bank.append(piece_in)
+        y2 = jnp.stack(bank, 0)
+        v_next = all_to_all(y2, which_axis, 0, 0)
+        return jnp.concatenate(v_next, 1)
+
     terms = jnp.dot(
-        hidden,
-        lax.all_gather(down_weight, "fsdp", axis=1, tiled=True),
-        preferred_element_type=jnp.float32,
+        hidden, process_sheet_in(down_weight, "fsdp"), preferred_element_type=jnp.float32
     )
     return lax.psum_scatter(
         terms.astype(jnp.bfloat16), ("dp", "tensor"), scatter_dimension=1, tiled=True

time: 567 us -> 512 us (0.903)
  waiting for transfers between devices: 332 us -> 268 us
  starting transfers between devices: 0.42 us -> 7.99 us
    all_gather x1 -> x0, waiting for transfers between devices: 46.1 us -> none  [feed_forward(): lax.all_gather(down_weight, 'fsdp', axis=1, tiled=True)]
    all_gather x1, waiting for transfers between devices: 49.9 us -> 40.7 us  [feed_forward(): lax.all_gather(ordered_cols, ('dp', 'tensor'), axis=1, tiled=True)]
    all_gather x1, waiting for transfers between devices: 51.6 us -> 44 us  [feed_forward(): lax.all_gather(up_weight, 'fsdp', axis=0, tiled=True)]
    all_to_all x0 -> x1, starting transfers between devices: none -> 7.61 us  [process_sheet_in(): v_next = all_to_all(y2, which_axis, 0, 0)]
    unnamed x8 -> x7, waiting for transfers between devices: 137 us -> 136 us
    unnamed x24 -> x27, local copies, waits for them, and re-layouts: 23.9 us -> 24 us
  transfers between devices with their start and end apart: 6 -> 6, of which waited for: 6 -> 5; matrix products, arithmetic and copies ran while one was open for 2% -> 3% of each run, Pallas kernels for 0% -> 0%
where the time goes in v1:
time: 512 us; the launch traced here: 511 us
  waiting for transfers between devices  268 us (52%)
  blocking collectives  92.4 us (18%)
  other arithmetic  46.5 us (9%)
  matrix products  43.7 us (9%)
  local copies, waits for them, and re-layouts  35.9 us (7%)
  between operations  13.3 us (3%)
  starting transfers between devices  7.99 us (2%)
    unnamed x7, waiting for transfers between devices  136 us
    all_gather x1, waiting for transfers between devices, feed_forward(): lax.all_gather(gate_weight, 'fsdp', axis=0, tiled=True)  47.7 us
    all_gather x1, waiting for transfers between devices, feed_forward(): lax.all_gather(up_weight, 'fsdp', axis=0, tiled=True)  44 us
    all_gather x1, waiting for transfers between devices, feed_forward(): lax.all_gather(ordered_cols, ('dp', 'tensor'), axis=1, tiled=True)  40.7 us
    unnamed x27, local copies, waits for them, and re-layouts  24 us
    all_gather x1, blocking collectives, body(): lax.all_gather(value_weight, 'fsdp', axis=0, tiled=True)  24 us
    scatter x1, other arithmetic, body(): return own_cols.at[row_order].set(mixed)  23.4 us
    all_gather x1, blocking collectives, body(): lax.all_gather(output_weight, 'fsdp', axis=1, tiled=True)  23.1 us
  transfers between devices with their start and end apart: 6, of which 5 were waited for; matrix products, arithmetic and copies ran while one was open for 3% of the time, Pallas kernels for 0%

profile of v1, /device:TPU:2, one launch (start us, length us, event | category | flops | bytes accessed | tf_op | source)
XLA Modules:
  0.0 510.8 jit_solution(6873906428694653952)
XLA Ops:
  6.5 5.1 %fusion.10 = f32[2048]{0:T(1024)S(1)} fusion(bf16[2048,2048]{1,0:T(8,128)(2,1)} %param.17), kind=kLoop, calls=%fused_computation.19 | loop fusion | flops 12580864 | bytes 8396800 | tf_op jit(solution)/shard_map/reduce_sum | solution.py:13
  11.7 24.0 %all_gather.23 = bf16[2048,128]{1,0:T(8,128)(2,1)S(1)} all-gather(bf16[128,128]{1,0:T(8,128)(2,1)S(1)} %copy-done.2), channel_id=1, replica_groups=mesh['dp'=8,'fsdp'=16,'tensor'=2] {'fsdp'}, dimensions={0}, use_global_device_ids=true | all-gather | bytes 557056 | tf_op jit(solution)/shard_map/all_gather | solution.py:97
  35.7 22.5 %all_gather.22 = bf16[2048,128]{1,0:T(8,128)(2,1)S(1)} all-gather(bf16[128,128]{1,0:T(8,128)(2,1)S(1)} %copy-done.3), channel_id=1, replica_groups=mesh['dp'=8,'fsdp'=16,'tensor'=2] {'fsdp'}, dimensions={0}, use_global_device_ids=true | all-gather | bytes 557056 | tf_op jit(solution)/shard_map/all_gather | solution.py:96
  58.2 8.6 %fusion.12 = bf16[2048,2048]{1,0:T(8,128)(2,1)} fusion(bf16[2048,2048]{1,0:T(8,128)(2,1)} %param.17, f32[2048]{0:T(1024)S(1)} %copy-done.8, f32[2048]{0:T(1024)S(1)} %add_rsqrt_fusion.1), kind=kLoop, calls=%fused_computation.21 | loop fusion | flops 16777216 | bytes 16793600 | tf_op jit(solution)/shard_map/convert_element_type | solution.py:14
  66.7 5.9 %convolution_convert_fusion.2 = bf16[2048,128]{1,0:T(8,128)(2,1)S(1)} fusion(bf16[2048,2048]{1,0:T(8,128)(2,1)} %fusion.12, bf16[2048,128]{1,0:T(8,128)(2,1)S(1)} %all_gather.23), kind=kOutput, calls=%fused_computation.31 | convolution fusion | flops 1074003968 | bytes 9437184 | tf_op jit(solution)/shard_map/dot_general | solution.py:101
  72.6 2.4 convolution_convert_fusion.3
  75.0 22.8 %all_gather.21 = bf16[2048,128]{1,0:T(8,128)(2,1)S(1)} all-gather(bf16[128,128]{1,0:T(8,128)(2,1)S(1)} %copy-done.4), channel_id=1, replica_groups=mesh['dp'=8,'fsdp'=16,'tensor'=2] {'fsdp'}, dimensions={0}, use_global_device_ids=true | all-gather | bytes 557056 | tf_op jit(solution)/shard_map/all_gather | solution.py:95
  97.8 2.4 convolution_convert_fusion.4
  100.3 17.5 %while.11 = (s32[]{:T(128)}, bf16[4,512,128]{2,1,0:T(8,128)(2,1)S(1)}, s32[4]{0:T(128)S(1)}, s32[2048]{0:T(1024)S(1)}, bf16[2048,128]{1,0:T(8,128)(2,1)S(1)}, /*...) while((s32[]{:T(128)}, ...), condition=%wide.region_4.5_spmd.clone, body=%wide.region_1.4_spmd.clone.sunk | while | flops 548470272 | bytes 13922487 | solution.py:43
  117.8 23.1 %all_gather.24 = bf16[128,2048]{1,0:T(8,128)(2,1)S(1)} all-gather(bf16[128,128]{1,0:T(8,128)(2,1)S(1)} %copy-done.5), channel_id=1, replica_groups=mesh['dp'=8,'fsdp'=16,'tensor'=2] {'fsdp'}, dimensions={1}, use_global_device_ids=true | all-gather | bytes 557056 | tf_op jit(solution)/shard_map/all_gather | solution.py:113
  140.8 5.6 %convolution_convert_fusion.1 = bf16[2048,2048]{1,0:T(8,128)(2,1)} fusion(bf16[2048,128]{1,0:T(8,128)(2,1)S(1)} %bitcast.38, bf16[128,2048]{1,0:T(8,128)(2,1)S(1)} %all_gather.24), kind=kOutput, calls=%fused_computation.28 | convolution fusion | flops 1077936128 | bytes 9437184 | tf_op jit(solution)/shard_map/dot_general | solution.py:111
  146.4 12.3 %copy.16 = bf16[2048,2048]{0,1:T(8,128)(2,1)} copy(bf16[2048,2048]{1,0:T(8,128)(2,1)} %convolution_convert_fusion.1) | data formatting | bytes 16777216
  159.4 71.6 %reduce-scatter.7.cloned.1.call-done = bf16[128,2048]{1,0:T(8,128)(2,1)} async-done(((bf16[2048,2048]{1,0:T(8,128)(2,1)}), bf16[128,2048]{1,0:T(8,128)(2,1)}) %reduce-scatter.7.cloned.1.call-update) | async-done | bytes 524304
  234.3 6.2 %gather_fusion = bf16[2048,128]{1,0:T(8,128)(2,1)S(1)} fusion(bf16[2048,128]{1,0:T(8,128)(2,1)S(1)} %get-tuple-element.79, s32[2048]{0:T(1024)S(1)} %get-tuple-element.83), kind=kCustom, calls=%fused_computation.clone | custom fusion | bytes 1056768 | tf_op jit(solution)/shard_map/jit(_take)/gather | solution.py:123
  244.7 7.6 %all-to-all-start = ((bf16[16,512,128]{1,2,0:T(8,128)(2,1)}), bf16[16,512,128]{1,2,0:T(8,128)(2,1)S(1)}, u32[]{:S(2)}, u32[]{:S(2)}) async-start(bf16[16,512,128]{1,2,0:T(8,128)(2,1)} %stack.2), calls=%async_computation | async-start | bytes 4194304 | tf_op jit(solution)/shard_map/all_to_all | solution.py:67
  252.5 40.7 %all-gather.4.cloned.1.call-done = bf16[1280,2048]{1,0:T(8,128)(2,1)} async-done(((bf16[1280,128]{1,0:T(8,128)(2,1)}), bf16[1280,2048]{1,0:T(8,128)(2,1)}) %all-gather.4.cloned.1.call-update) | async-done | bytes 5242896 | tf_op jit(solution)/shard_map/all_gather | solution.py:48
  293.3 3.6 fusion.13
  296.9 47.7 %all-gather.6.cloned.1.call-done = bf16[2048,512]{1,0:T(8,128)(2,1)} async-done(((bf16[128,512]{1,0:T(8,128)(2,1)}), bf16[2048,512]{1,0:T(8,128)(2,1)}) %all-gather.6.cloned.1.call-update) | async-done | bytes 2097168 | tf_op jit(solution)/shard_map/all_gather | solution.py:52
  344.5 7.6 %fusion.18 = f32[1280,512]{1,0:T(8,128)} fusion(bf16[2048,512]{1,0:T(8,128)(2,1)} %all-gather.6.cloned.1.call-done, bf16[1280,2048]{1,0:T(8,128)(2,1)} %all-gather.4.cloned.1.call-done, f32[2048]{0:T(1024)S(1)} %copy-done.9, f32[1280]{0:T(1024)S(1)} %add_rsqrt_fusion), kind=kOutput, calls=%fused_computation.34 | convolution fusion | flops 2694840320 | bytes 9974784 | tf_op jit(solution)/shard_map/dot_general | solution.py:50
  352.2 44.0 %all-gather.8.cloned.1.call-done = bf16[2048,512]{1,0:T(8,128)(2,1)} async-done(((bf16[128,512]{1,0:T(8,128)(2,1)}), bf16[2048,512]{1,0:T(8,128)(2,1)}) %all-gather.8.cloned.1.call-update) | async-done | bytes 2097168 | tf_op jit(solution)/shard_map/all_gather | solution.py:57
  396.2 10.6 %convolution_convert_fusion = bf16[1280,2048]{1,0:T(8,128)(2,1)} fusion(bf16[512,2048]{0,1:T(8,128)(2,1)S(1)} %bitcast.37, bf16[2048,512]{1,0:T(8,128)(2,1)} %all-gather.8.cloned.1.call-done, f32[1280,512]{1,0:T(8,128)} %fusion.18, bf16[1280,2048]{1,0:T(8,128)(2,1)} %all-gather.4.cloned.1.call-done, f32[2048]{0:T(1024)S(1)} %copy-done.9, ...), kind=kOutput, calls=%fused_computation.27 | convolution fusion | flops 5385748480 | bytes 17314816 | tf_op jit(solution)/shard_map/dot_general | solution.py:70
  406.8 7.9 %copy.18 = bf16[1280,2048]{0,1:T(8,128)(2,1)} copy(bf16[1280,2048]{1,0:T(8,128)(2,1)} %convolution_convert_fusion) | data formatting | bytes 10485760
  416.5 63.2 %reduce-scatter.9.cloned.1.call-done = bf16[128,1280]{1,0:T(8,128)(2,1)} async-done(((bf16[2048,1280]{1,0:T(8,128)(2,1)}), bf16[128,1280]{1,0:T(8,128)(2,1)}) %reduce-scatter.9.cloned.1.call-update) | async-done | bytes 327696
  480.9 23.4 %scatter_custom_fusion = bf16[2048,128]{1,0:T(8,128)(2,1)} fusion(bf16[2048,128]{1,0:T(8,128)(2,1)} %get-tuple-element.80, s32[2048]{0:T(1024)S(1)} %get-tuple-element.84, bf16[768,128]{1,0:T(8,128)(2,1)S(1)} %slice.13, bf16[]{:T(256)} %constant.75, bf16[1280,128]{1,0:T(8,128)(2,1)S(1)} %add_convert_fusion.1, pred[2048]{0:T(1024)(128)(4,1)S(1)} %compare_and_fusion, ...), kind=kCustom, calls=%fused_computation.39 | custom fusion | flops 1572864 | bytes 1585156 | tf_op jit(solution)/shard_map/scatter | solution.py:135
  (74 shorter events, 26.3 us)
Async XLA Ops:
  6.5 5.1 %copy-start.2 = (bf16[128,128]{1,0:T(8,128)(2,1)S(1)}, bf16[128,128]{1,0:T(8,128)(2,1)}, u32[]{:S(2)}) copy-start(bf16[128,128]{1,0:T(8,128)(2,1)} %param.25) | copy-start | bytes 98308
  6.5 29.1 %copy-start.3 = (bf16[128,128]{1,0:T(8,128)(2,1)S(1)}, bf16[128,128]{1,0:T(8,128)(2,1)}, u32[]{:S(2)}) copy-start(bf16[128,128]{1,0:T(8,128)(2,1)} %param.24) | copy-start | bytes 98308
  6.5 51.6 %copy-start.8 = (f32[2048]{0:T(1024)S(1)}, f32[2048]{0:T(1024)}, u32[]{:S(2)}) copy-start(f32[2048]{0:T(1024)} %param.21) | copy-start | bytes 24580
  6.5 224.5 %reduce-scatter.7.cloned.1.call-start = ((), (), s32[]{:S(2)}) async-start(), calls=%async_computation.6 | async-start | bytes 8912896
  66.7 5.9 %copy-start = (bf16[2048,2048]{1,0:T(8,128)(2,1)S(1)}, bf16[2048,2048]{1,0:T(8,128)(2,1)}, u32[]{:S(2)}) copy-start(bf16[2048,2048]{1,0:T(8,128)(2,1)} %fusion.12) | copy-start | bytes 25165828
  72.6 2.4 copy-start.4
  97.8 2.4 copy-start.7
  100.3 17.5 %copy-start.5 = (bf16[128,128]{1,0:T(8,128)(2,1)S(1)}, bf16[128,128]{1,0:T(8,128)(2,1)}, u32[]{:S(2)}) copy-start(bf16[128,128]{1,0:T(8,128)(2,1)} %param.26) | copy-start | bytes 98308
  158.7 0.7 copy-start.6
  158.7 84.2 %copy-start.1 = (bf16[512,128]{1,0:T(8,128)(2,1)S(1)}, bf16[512,128]{1,0:T(8,128)(2,1)}, u32[]{:S(2)}) copy-start(bf16[512,128]{1,0:T(8,128)(2,1)} %param.29) | copy-start | bytes 393220
  158.7 134.5 %all-gather.4.cloned.1.call-start = ((), (), s32[]{:S(2)}) async-start(), calls=%async_computation.3 | async-start | bytes 5570560 | tf_op jit(solution)/shard_map/all_gather | solution.py:48
  241.6 102.9 %all-gather.6.cloned.1.call-start = ((), (), s32[]{:S(2)}) async-start(), calls=%async_computation.4 | async-start | bytes 2228224 | tf_op jit(solution)/shard_map/all_gather | solution.py:52
  242.4 153.8 %all-gather.8.cloned.1.call-start = ((), (), s32[]{:S(2)}) async-start(), calls=%async_computation.5 | async-start | bytes 2228224 | tf_op jit(solution)/shard_map/all_gather | solution.py:57
  244.7 99.9 %copy-start.9 = (f32[2048]{0:T(1024)S(1)}, f32[2048]{0:T(1024)}, u32[]{:S(2)}) copy-start(f32[2048]{0:T(1024)} %param.22) | copy-start | bytes 24580
  244.7 107.5 %all-to-all-start = ((bf16[16,512,128]{1,2,0:T(8,128)(2,1)}), bf16[16,512,128]{1,2,0:T(8,128)(2,1)S(1)}, u32[]{:S(2)}, u32[]{:S(2)}) async-start(bf16[16,512,128]{1,2,0:T(8,128)(2,1)} %stack.2), calls=%async_computation | async-start | bytes 4194304 | tf_op jit(solution)/shard_map/all_to_all | solution.py:67
  252.3 227.4 %reduce-scatter.9.cloned.1.call-start = ((), (), s32[]{:S(2)}) async-start(), calls=%async_computation.7 | async-start | bytes 5570560
  414.6 0.7 copy-start.10
Sparse Core Ops, SparseCore 0:
  158.8 72.1 reduce-scatter.6
  241.7 51.4 all-gather.3
  295.7 48.7 all-gather.5
  346.8 49.3 all-gather.7
  414.8 64.8 reduce-scatter.8
